TPU v7x, 512 devices: a whole 4x4x16 slice. The times are simulated.
512 devices in a mesh: win: 64 (over y, z), state: 8 (over x, core).
Axes of the slice: x: 4, y: 4, z: 16, core: 2. Of those that a mesh axis runs over, the one named last changes fastest.
Arguments:
- anomalies: float32 [64, 2048, 256], P('win', 'state'), may hold values from -12 to 12
- mean_state: float32 [64, 2048], P('win', 'state'), may hold values from -6 to 6
- obs_rows: int32 [64, 1024], P('win', 'state'), may hold values from 0 to 255
- obs_precision: float32 [64, 1024], P('win', 'state'), may hold values from 0.001953125 to 0.01953125
Outputs:
- updated: float32 [64, 2048, 256], P('win', 'state')
Inputs may be any that keep to these rules, and one draw needn't show every extreme that they name: Observation j of window w reads state row (j // 128) * 256 + obs_rows[w, j], a row of the same block of 256 rows.
All inputs are finite; a program needn't handle non-finite values.
Results may differ from a plain program's by a relative error of at most 0.0003.
Values sent between devices are 32-bit elements; how exact they have to be, the bound alone decides.
No kernel may reach another device: no remote copies, remote signals or barrier semaphores. Data moves between devices by JAX's collectives and lax.ppermute only.
A program may use at most 128 MiB of HBM per device.

v0:
```python
import jax
import jax.numpy as jnp
from jax import lax
from jax.sharding import PartitionSpec as P

NS_STEPS = 3
PRECISE = lax.Precision.HIGHEST


def carried_in(value, axis, join, neutral):
    count, mine = (lax.axis_size(axis), lax.axis_index(axis))
    pieces = lax.all_gather(value, axis)
    pieces = pieces[::-1]
    mine = count - 1 - mine
    running = jnp.full_like(value, 0) + jnp.asarray(neutral, value.dtype)

    def step(position, running):
        longer = join(running, pieces[position])
        return jnp.where(position < mine, longer, running)

    return lax.fori_loop(0, count - 1, step, running)


def high_dot(left, right):
    return jnp.dot(left, right, precision=PRECISE, preferred_element_type=jnp.float32)


def inverse_root(gram_matrix):
    members = gram_matrix.shape[0]
    unit_matrix = jnp.eye(members, dtype=jnp.float32)
    system = unit_matrix + gram_matrix
    frob_scale = jnp.sqrt(jnp.sum(system * system))
    root_iter = system / frob_scale
    factor = 1.5 * unit_matrix - 0.5 * root_iter
    inverse = factor
    root_iter = high_dot(root_iter, factor)
    for ns_index in range(1, NS_STEPS):
        factor = 1.5 * unit_matrix - 0.5 * high_dot(inverse, root_iter)
        if ns_index + 1 < NS_STEPS:
            root_iter = high_dot(root_iter, factor)
        inverse = high_dot(factor, inverse)
    return inverse * (members / jnp.trace(inverse))


def gram_terms(current, mean_state, obs_rows, obs_precision):
    row_count = current.shape[1]
    members = current.shape[2]
    positions = jnp.arange(row_count, dtype=jnp.int32)
    selector = (obs_rows[:, :, None] == positions[None, None, :]).astype(jnp.float32)
    picked = jnp.einsum("wor,wrm->wom", selector, current, precision=PRECISE)
    base_value = jnp.einsum("wor,wr->wo", selector, mean_state, precision=PRECISE)
    predicted = jnp.tanh(base_value[:, :, None] + picked)
    centred = (predicted - jnp.mean(predicted, axis=2, keepdims=True)) * jnp.sqrt(obs_precision)[
        :, :, None
    ]
    return jnp.einsum("wom,won->wmn", centred, centred, precision=PRECISE) / (members - 1)


def combine_later(earlier, later_part):
    return high_dot(later_part, earlier)


def shards(anomalies, mean_state, obs_rows, obs_precision):
    current = anomalies
    window_count = anomalies.shape[0]
    members = anomalies.shape[2]
    unit_matrix = jnp.eye(members, dtype=jnp.float32)
    local_grams = gram_terms(current, mean_state, obs_rows, obs_precision)
    summed = lax.psum(local_grams, "state")
    transforms = [inverse_root(summed[0])]
    running = transforms[window_count - 1]
    later_product = carried_in(running, "win", combine_later, unit_matrix)
    current = jnp.stack([high_dot(current[0], high_dot(running, later_product))])
    return current


def solution(mesh):
    placed = (P("win", "state", None), P("win", "state"), P("win", "state"), P("win", "state"))
    return jax.shard_map(
        shards, mesh=mesh, in_specs=placed, out_specs=P("win", "state", None), check_vma=False
    )
```

profile of v0, /device:TPU:1, one launch (start us, length us, event | category | flops | bytes accessed | tf_op | source)
XLA Modules:
  0.0 400.5 jit_solution(16687633099318122900)
XLA Ops:
  10.5 79.7 %all-reduce.2.cloned.1.call-done = f32[1,256,256]{2,1,0:T(8,128)} async-done(((f32[1,256,256]{2,1,0:T(8,128)}), f32[1,256,256]{2,1,0:T(8,128)}) %all-reduce.2.cloned.1.call-update) | async-done | bytes 262160 | tf_op jit(solution)/shard_map/psum | solution.py:69
  90.2 1.6 multiply_reduce_fusion
  92.5 1.5 fusion.7
  93.9 1.4 fusion.4
  95.7 1.4 fusion.32
  99.9 192.8 %all-gather.3.cloned.1.call-done = f32[16384,256]{1,0:T(8,128)} async-done(((f32[256,256]{1,0:T(8,128)}), f32[16384,256]{1,0:T(8,128)}) %all-gather.3.cloned.1.call-update) | async-done | bytes 16777232 | tf_op jit(solution)/shard_map/all_gather | solution.py:12
  292.8 11.5 %rev.3 = f32[64,256,256]{2,1,0:T(8,128)} reverse(f32[64,256,256]{2,1,0:T(8,128)} %bitcast.62), dimensions={0} | reverse | bytes 33554432 | tf_op jit(solution)/shard_map/rev | solution.py:13
  304.3 87.5 %while.13 = (s32[]{:T(128)}, f32[256,256]{1,0:T(8,128)S(1)}, s32[]{:T(128)}, f32[64,256,256]{2,1,0:T(8,128)}, s32[]{:T(128)}) while((s32[]{:T(128)}, f32[256,256]{1,0:T(8,128)S(1)}, s32[]{:T(128)}, f32[64,256,256]{2,1,0:T(8,128)}, s32[]{:T(128)}) %tuple.30), condition=%wide.region_5.6_spmd, body=%wide.region_4.5_spmd.sunk | while | flops 201392128 | bytes 1573447 | solution.py:21
  305.7 1.3 convolution_select_fusion.2
  307.1 1.3 convolution_select_fusion.2
  308.4 1.3 convolution_select_fusion.2
  309.8 1.3 convolution_select_fusion.2
  311.2 1.3 convolution_select_fusion.2
  314.0 1.3 convolution_select_fusion.2
  315.4 1.3 convolution_select_fusion.2
  318.2 1.3 convolution_select_fusion.2
  319.6 1.3 convolution_select_fusion.2
  322.3 1.3 convolution_select_fusion.2
  323.7 1.3 convolution_select_fusion.2
  325.1 1.3 convolution_select_fusion.2
  326.5 1.3 convolution_select_fusion.2
  327.9 1.3 convolution_select_fusion.2
  329.3 1.3 convolution_select_fusion.2
  330.7 1.3 convolution_select_fusion.2
  (131 shorter events, 72.2 us)
Async XLA Ops:
  6.5 1.0 copy-start
  6.5 83.6 %all-reduce.2.cloned.1.call-start = ((), (), s32[]{:S(2)}) async-start(), calls=%async_computation | async-start | bytes 524288 | tf_op jit(solution)/shard_map/psum | solution.py:69
  10.4 282.3 %all-gather.3.cloned.1.call-start = ((), (), s32[]{:S(2)}) async-start(), calls=%async_computation.1 | async-start | bytes 17039360 | tf_op jit(solution)/shard_map/all_gather | solution.py:12
  292.8 99.0 %copy-start.1 = (f32[256,256]{1,0:T(8,128)S(1)}, f32[256,256]{1,0:T(8,128)}, u32[]{:S(2)}) copy-start(f32[256,256]{1,0:T(8,128)} %broadcast_multiply_fusion) | copy-start | bytes 786436
Sparse Core Ops, SparseCore 0:
  10.6 79.5 all-reduce.1
  100.0 192.7 all-gather.2
where the time goes:
time: 403 us; the launch traced here: 400 us
  waiting for transfers between devices  273 us (68%)
  matrix products  94.2 us (23%)
  between operations  14.9 us (4%)
  local copies, waits for them, and re-layouts  14.2 us (4%)
    all_gather x1, waiting for transfers between devices, carried_in(): pieces = lax.all_gather(value, axis)  193 us
    dot_general x71, matrix products, high_dot(): jnp.dot(left, right, precision=PRECISE, preferred_element_type=jnp.float32)  91 us
    psum x1, waiting for transfers between devices, shards(): summed = lax.psum(local_grams, 'state')  79.7 us
    rev x1, local copies, waits for them, and re-layouts, carried_in(): pieces = pieces[::-1]  11.5 us
  transfers between devices with their start and end apart: 2, of which 2 were waited for; matrix products, arithmetic and copies ran while one was open for 0% of the time, Pallas kernels for 0%

commit v1 on v0

--- a/solution.py
+++ b/solution.py
@@ -66,7 +66,7 @@
     members = anomalies.shape[2]
     unit_matrix = jnp.eye(members, dtype=jnp.float32)
     local_grams = gram_terms(current, mean_state, obs_rows, obs_precision)
-    summed = lax.psum(local_grams, "state")
+    summed = jnp.sum(lax.all_gather(local_grams, "state"), axis=0)
     transforms = [inverse_root(summed[0])]
     running = transforms[window_count - 1]
     later_product = carried_in(running, "win", combine_later, unit_matrix)

time: 403 us -> 359 us (0.89)
  waiting for transfers between devices: 273 us -> 231 us
    psum x1 -> x0, waiting for transfers between devices: 79.7 us -> none  [shards(): summed = lax.psum(local_grams, 'state')]
    all_gather x0 -> x1, waiting for transfers between devices: none -> 38.7 us  [shards(): summed = jnp.sum(lax.all_gather(local_grams, 'state'), axis=0)]
where the time goes in v1:
time: 359 us; the launch traced here: 357 us
  waiting for transfers between devices  231 us (64%)
  matrix products  91.2 us (25%)
  between operations  14.9 us (4%)
  local copies, waits for them, and re-layouts  14.2 us (4%)
    all_gather x1, waiting for transfers between devices, carried_in(): pieces = lax.all_gather(value, axis)  192 us
    dot_general x71, matrix products, high_dot(): jnp.dot(left, right, precision=PRECISE, preferred_element_type=jnp.float32)  88.1 us
    all_gather x1, waiting for transfers between devices, shards(): summed = jnp.sum(lax.all_gather(local_grams, 'state'), axis=0)  38.7 us
    rev x1, local copies, waits for them, and re-layouts, carried_in(): pieces = pieces[::-1]  11.5 us
  transfers between devices with their start and end apart: 2, of which 2 were waited for; matrix products, arithmetic and copies ran while one was open for 0% of the time, Pallas kernels for 0%

profile of v1, /device:TPU:1, one launch (start us, length us, event | category | flops | bytes accessed | tf_op | source)
XLA Modules:
  0.0 356.9 jit_solution(17564962396289462433)
XLA Ops:
  10.5 38.7 %all-gather.5.cloned.1.call-done = f32[2048,256]{1,0:T(8,128)} async-done(((f32[256,256]{1,0:T(8,128)}), f32[2048,256]{1,0:T(8,128)}) %all-gather.5.cloned.1.call-update) | async-done | bytes 2097168 | tf_op jit(solution)/shard_map/all_gather | solution.py:69
  49.2 1.8 reduce.3
  56.9 192.4 %all-gather.7.cloned.1.call-done = f32[16384,256]{1,0:T(8,128)} async-done(((f32[256,256]{1,0:T(8,128)}), f32[16384,256]{1,0:T(8,128)}) %all-gather.7.cloned.1.call-update) | async-done | bytes 16777232 | tf_op jit(solution)/shard_map/all_gather | solution.py:12
  249.2 11.5 %rev.3 = f32[64,256,256]{2,1,0:T(8,128)} reverse(f32[64,256,256]{2,1,0:T(8,128)} %bitcast.62), dimensions={0} | reverse | bytes 33554432 | tf_op jit(solution)/shard_map/rev | solution.py:13
  260.7 87.5 %while.13 = (s32[]{:T(128)}, f32[256,256]{1,0:T(8,128)S(1)}, s32[]{:T(128)}, f32[64,256,256]{2,1,0:T(8,128)}, s32[]{:T(128)}) while((s32[]{:T(128)}, f32[256,256]{1,0:T(8,128)S(1)}, s32[]{:T(128)}, f32[64,256,256]{2,1,0:T(8,128)}, s32[]{:T(128)}) %tuple.30), condition=%wide.region_5.6_spmd, body=%wide.region_4.5_spmd.sunk | while | flops 201392128 | bytes 1573447 | solution.py:21
  262.1 1.3 convolution_select_fusion.2
  263.5 1.3 convolution_select_fusion.2
  264.9 1.3 convolution_select_fusion.2
  266.3 1.3 convolution_select_fusion.2
  267.7 1.3 convolution_select_fusion.2
  269.1 1.3 convolution_select_fusion.2
  270.5 1.3 convolution_select_fusion.2
  271.9 1.3 convolution_select_fusion.2
  274.6 1.3 convolution_select_fusion.2
  276.0 1.3 convolution_select_fusion.2
  278.8 1.3 convolution_select_fusion.2
  280.2 1.3 convolution_select_fusion.2
  283.0 1.3 convolution_select_fusion.2
  284.4 1.3 convolution_select_fusion.2
  285.8 1.3 convolution_select_fusion.2
  287.2 1.3 convolution_select_fusion.2
  288.5 1.3 convolution_select_fusion.2
  289.9 1.3 convolution_select_fusion.2
  291.3 1.3 convolution_select_fusion.2
  (132 shorter events, 70.1 us)
Async XLA Ops:
  6.5 1.0 copy-start
  6.5 42.7 %all-gather.5.cloned.1.call-start = ((), (), s32[]{:S(2)}) async-start(), calls=%async_computation | async-start | bytes 2359296 | tf_op jit(solution)/shard_map/all_gather | solution.py:69
  10.4 238.8 %all-gather.7.cloned.1.call-start = ((), (), s32[]{:S(2)}) async-start(), calls=%async_computation.1 | async-start | bytes 17039360 | tf_op jit(solution)/shard_map/all_gather | solution.py:12
  249.2 99.0 %copy-start.1 = (f32[256,256]{1,0:T(8,128)S(1)}, f32[256,256]{1,0:T(8,128)}, u32[]{:S(2)}) copy-start(f32[256,256]{1,0:T(8,128)} %broadcast_multiply_fusion) | copy-start | bytes 786436
Sparse Core Ops, SparseCore 0:
  10.6 38.6 all-gather.4
  57.0 192.2 all-gather.6
